TPU v7x, 256 devices: a whole 4x4x8 slice. The times are simulated.
256 devices in a mesh: wide: 128 (over x, y, z_lo, core), head: 2 (over z_hi).
Axes of the slice: x: 4, y: 4, z: 8 (z_hi: 2, z_lo: 4; z = z_hi * 4 + z_lo), core: 2. Of those that a mesh axis runs over, the one named last changes fastest.
Arguments:
- branch_query: bfloat16 [512, 8192], P('wide', 'head'), may hold values from -6 to 6
- key_new: bfloat16 [512, 1024], P('wide', 'head'), may hold values from -6 to 6
- value_new: bfloat16 [512, 1024], P('wide', 'head'), may hold values from -6 to 6
- pool_pages: bfloat16 [2, 8192, 16, 1024], P(None, 'wide', None, 'head'), may hold values from -6 to 6
- page_table: int32 [512, 16], P('wide'), may hold values from 0 to 63, as said below
- tail_length: int32 [512], P('wide'), may hold values from 1 to 256
- parent_row: int32 [512], P('wide'), may hold values from 0 to 511, as said below
- residual: bfloat16 [512, 8192], P(('wide', 'head')), may hold values from -6 to 6
- norm_gain: float32 [8192], replicated, may hold values from 0.5 to 1.5
- gate_blocks: bfloat16 [128, 32, 128, 128], P('wide'), may hold values from -0.09375 to 0.09375
- up_blocks: bfloat16 [128, 32, 128, 128], P('wide'), may hold values from -0.09375 to 0.09375
- gate_up_keep: int32 [128, 32], P('wide'), may hold values from 0 to 63, as said below
- gate_scale: float32 [128, 32], P('wide'), may hold values from 0.5 to 2
- up_scale: float32 [128, 32], P('wide'), may hold values from 0.5 to 2
- down_blocks: bfloat16 [128, 32, 128, 128], P('wide'), may hold values from -0.0625 to 0.0625
- down_keep: int32 [128, 32], P('wide'), may hold values from 0 to 63, as said below
- down_scale: float32 [128, 32], P('wide'), may hold values from 0.5 to 2
Outputs:
- layer_out: bfloat16 [512, 8192], P(('wide', 'head'))
Inputs may be any that keep to these rules, and one draw needn't show every extreme that they name: parent_row never falls with the branch index, and parent_row[b] <= b and parent_row[b] > b - 4. `page_table`: the entries of the 4 rows held by one index of wide name each of that index's 64 pages once. `gate_up_keep`: each row names 32 different blocks. `down_keep`: each row names 32 different blocks.
All inputs are finite; a program needn't handle non-finite values.
Results may differ from a plain program's by a relative error of at most 0.017.
Values may be sent and summed in bfloat16 or wider, within the bound.
A program may use at most 64 MiB of HBM per device.

v0:
```python
import math
import jax
import jax.numpy as jnp
from jax import lax
from jax.sharding import PartitionSpec as P

HD = 128
BLK = 128


def shifted(block, axis, distance):
    devices = range(lax.axis_size(axis))
    route = [(i - distance, i) for i in devices if i - distance in devices]
    return lax.ppermute(block, axis, route)


def attend(branch_query, key_new, value_new, child_tails, child_length):
    row_count = branch_query.shape[0]
    groups = key_new.shape[1] // HD
    per_group = branch_query.shape[1] // (groups * HD)
    tail_size = child_tails.shape[2]
    queries = branch_query.reshape(row_count, groups, per_group, HD)
    tail_keys = child_tails[0].reshape(row_count, tail_size, groups, HD)
    tail_values = child_tails[1].reshape(row_count, tail_size, groups, HD)
    own_keys = key_new.reshape(row_count, groups, HD)
    own_values = value_new.reshape(row_count, groups, HD)
    factor = 1.0 / math.sqrt(HD)
    tail_scores = (
        jnp.einsum("rgjd,rtgd->rgjt", queries, tail_keys, preferred_element_type=jnp.float32)
        * factor
    )
    own_scores = (
        jnp.einsum("rgjd,rgd->rgj", queries, own_keys, preferred_element_type=jnp.float32) * factor
    )
    live_mask = (jnp.arange(tail_size, dtype=jnp.float32)[None, :] < child_length[:, None])[
        :, None, None, :
    ]
    top_score = jnp.maximum(jnp.max(jnp.where(live_mask, tail_scores, -1e30), axis=-1), own_scores)
    tail_exp = jnp.where(live_mask, jnp.exp(tail_scores - top_score[..., None]), 0.0)
    own_exp = jnp.exp(own_scores - top_score)
    totals = jnp.sum(tail_exp, axis=-1) + own_exp
    tail_weights = (tail_exp / totals[..., None]).astype(jnp.bfloat16)
    own_weights = (own_exp / totals).astype(jnp.bfloat16)
    mixture = jnp.einsum(
        "rgjt,rtgd->rgjd", tail_weights, tail_values, preferred_element_type=jnp.float32
    )
    mixture = mixture + own_weights[..., None].astype(jnp.float32) * own_values[
        :, :, None, :
    ].astype(jnp.float32)
    return mixture.reshape(row_count, -1).astype(jnp.bfloat16)


def ffn_terms(picked, gate_blocks, up_blocks, gate_scale, up_scale, down_blocks, down_scale):
    gate_part = jnp.einsum(
        "rkd,kdf->rkf", picked, gate_blocks[0], preferred_element_type=jnp.float32
    )
    up_part = jnp.einsum("rkd,kdf->rkf", picked, up_blocks[0], preferred_element_type=jnp.float32)
    gate_sum = jnp.sum(gate_part * gate_scale[0][None, :, None], axis=1)
    up_sum = jnp.sum(up_part * up_scale[0][None, :, None], axis=1)
    hidden = (jax.nn.silu(gate_sum) * up_sum).astype(jnp.bfloat16)
    return (
        jnp.einsum("rf,kfe->rke", hidden, down_blocks[0], preferred_element_type=jnp.float32)
        * down_scale[0][None, :, None]
    )


def per_device(
    branch_query,
    key_new,
    value_new,
    pool_pages,
    page_table,
    tail_length,
    parent_row,
    residual,
    norm_gain,
    gate_blocks,
    up_blocks,
    gate_up_keep,
    gate_scale,
    up_scale,
    down_blocks,
    down_keep,
    down_scale,
):
    row_count = branch_query.shape[0]
    tail_size = page_table.shape[1] * pool_pages.shape[2]
    own_tails = pool_pages[:, page_table].reshape(2, row_count, tail_size, pool_pages.shape[3])
    own_length = tail_length.astype(jnp.bfloat16)
    prior_tails, prior_length = shifted((own_tails, own_length), "wide", 1)
    both_tails = jnp.concatenate([prior_tails, own_tails], axis=1)
    both_length = jnp.concatenate([prior_length, own_length]).astype(jnp.float32)
    local_parent = parent_row - (lax.axis_index("wide") - 1) * row_count
    child_tails = both_tails[:, local_parent]
    child_length = both_length[local_parent]
    attention = attend(branch_query, key_new, value_new, child_tails, child_length)
    head_rows = lax.all_to_all(attention, "head", split_axis=0, concat_axis=1, tiled=True)
    middle = residual.astype(jnp.float32) + head_rows.astype(jnp.float32)
    normed = (
        middle * lax.rsqrt(jnp.mean(middle * middle, axis=-1, keepdims=True) + 1e-05) * norm_gain
    ).astype(jnp.bfloat16)
    keep_lists = lax.all_gather(
        jnp.concatenate([gate_up_keep, down_keep], axis=1), "wide", axis=0, tiled=True
    )
    keep = gate_up_keep.shape[1]
    in_keep, out_keep = (keep_lists[:, :keep], keep_lists[:, keep:])
    feature_blocks = normed.shape[1] // BLK
    normed_blocks = normed.reshape(normed.shape[0], feature_blocks, BLK)
    outgoing = jnp.swapaxes(normed_blocks[:, in_keep], 0, 1)
    picked = lax.all_to_all(outgoing, "wide", split_axis=0, concat_axis=0, tiled=True)
    picked = picked.reshape(-1, keep, BLK)
    contrib = ffn_terms(
        picked, gate_blocks, up_blocks, gate_scale, up_scale, down_blocks, down_scale
    ).astype(jnp.bfloat16)
    contrib = contrib.reshape(-1, normed.shape[0], keep, BLK)
    arrived = lax.all_to_all(contrib, "wide", split_axis=0, concat_axis=0, tiled=True)
    senders = arrived.shape[0]
    placement = (
        out_keep.reshape(senders * keep, 1) == jnp.arange(feature_blocks, dtype=jnp.int32)[None, :]
    ).astype(jnp.bfloat16)
    flat = jnp.swapaxes(arrived, 0, 1).reshape(normed.shape[0], senders * keep, BLK)
    ffn_share = jnp.einsum(
        "rsd,sb->rbd", flat, placement, preferred_element_type=jnp.float32
    ).reshape(normed.shape[0], -1)
    return (middle + ffn_share).astype(jnp.bfloat16)


def solution(mesh):
    placed = (
        P("wide", "head"),
        P("wide", "head"),
        P("wide", "head"),
        P(None, "wide", None, "head"),
        P("wide", None),
        P("wide"),
        P("wide"),
        P(("wide", "head"), None),
        P(),
        P("wide", None, None, None),
        P("wide", None, None, None),
        P("wide", None),
        P("wide", None),
        P("wide", None),
        P("wide", None, None, None),
        P("wide", None),
        P("wide", None),
    )
    return jax.shard_map(
        per_device, mesh=mesh, in_specs=placed, out_specs=P(("wide", "head"), None), check_vma=False
    )
```

profile of v0, /device:TPU:1, one launch (start us, length us, event | category | flops | bytes accessed | tf_op | source)
XLA Modules:
  0.0 395.7 jit_solution(13125555480860348929)
XLA Ops:
  0.0 0.8 compare_select_fusion.1
  0.8 0.1 reshape.96
  0.9 0.7 copy-done
  1.6 2.0 gather_fusion.1
  3.6 0.0 copy-start.12
  3.6 0.0 copy-start.13
  3.7 3.2 copy.29
  6.8 4.9 %collective-permute-start.1 = (bf16[2,4,256,512]{3,2,1,0:T(8,128)(2,1)}, bf16[2,4,256,512]{3,2,1,0:T(8,128)(2,1)}, u32[]{:S(2)}, u32[]{:S(2)}) collective-permute-start(bf16[2,4,256,512]{3,2,1,0:T(8,128)(2,1)} %bitcast.2), channel_id=1, source_target_pairs={{0,2},{2,4},{4,6},{6,8},{8,10},{10,12},{12,14},{14,16},{16,18},{18... | collective-permute-start | bytes 6291464 | tf_op jit(solution)/shard_map/ppermute | solution.py:14
  11.8 1.9 collective-permute-start
  13.8 0.1 add_bitcast_fusion
  13.9 191.1 %all-gather = s32[128,1,64]{2,1,0:T(1,128)S(1)} all-gather(s32[1,1,64]{2,1,0:T(1,128)S(1)} %add_bitcast_fusion), channel_id=1, replica_groups=mesh['wide'=128,'head'=2] {'wide'}, dimensions={0}, use_global_device_ids=true | all-gather | bytes 33024 | tf_op jit(solution)/shard_map/all_gather | solution.py:102
  204.9 0.1 fusion.26
  205.0 0.1 reshape.112
  205.2 0.1 fusion.15
  205.3 0.1 maximum_convert_fusion
  205.4 0.6 gather_fusion
  206.0 0.1 iota_compare_fusion.1
  206.1 4.5 %pad_maximum_fusion = bf16[2,8,256,512]{3,2,1,0:T(8,128)(2,1)} fusion(bf16[2,4,256,512]{3,2,1,0:T(8,128)(2,1)} %bitcast.2, bf16[2,4,256,512]{3,2,1,0:T(8,128)(2,1)} %collective-permute-done.1), kind=kLoop, calls=%fused_computation.4 | loop fusion | flops 2097152 | bytes 8388608 | tf_op jit(solution)/shard_map/concatenate | solution.py:91
  210.6 4.2 %gather_fusion.2 = bf16[4,2,256,512]{3,2,1,0:T(8,128)(2,1)} fusion(bf16[2,8,256,512]{3,2,1,0:T(8,128)(2,1)} %pad_maximum_fusion, s32[1024]{0:T(1024)S(1)} %pad_clamp_fusion.1), kind=kCustom, calls=%fused_computation.2 | custom fusion | bytes 4194320 | tf_op jit(solution)/shard_map/gather | solution.py:94
  214.8 2.7 fusion.25
  217.5 1.3 copy.32
  218.8 1.5 copy.30
  220.3 0.3 select_reduce_fusion
  220.7 0.2 bitcast_reduce_fusion
  220.9 1.6 fusion
  222.5 0.6 convert_element_type.68
  223.2 6.4 %all-to-all-start = ((bf16[2,2,4096]{2,1,0:T(2,128)(2,1)}), bf16[2,2,4096]{2,1,0:T(2,128)(2,1)S(1)}, u32[]{:S(2)}, u32[]{:S(2)}) async-start(bf16[2,2,4096]{2,1,0:T(2,128)(2,1)} %convert_element_type.68), calls=%async_computation | async-start | bytes 65536 | tf_op jit(solution)/shard_map/all_to_all | solution.py:97
  229.6 6.7 %all-to-all-done = bf16[2,2,4096]{2,1,0:T(2,128)(2,1)S(1)} async-done(((bf16[2,2,4096]{2,1,0:T(2,128)(2,1)}), bf16[2,2,4096]{2,1,0:T(2,128)(2,1)S(1)}, u32[]{:S(2)}, u32[]{:S(2)}) %all-to-all-start) | async-done | bytes 32800 | tf_op jit(solution)/shard_map/all_to_all | solution.py:97
  236.3 0.2 multiply_reduce_fusion.2
  236.5 0.1 fusion.18
  236.6 26.9 %gather_fusion.3 = bf16[4096,2,128]{2,1,0:T(2,128)(2,1)} fusion(bf16[2,64,128]{2,0,1:T(2,128)(2,1)S(1)} %fusion.18, s32[4096]{0:T(1024)S(1)} %broadcast_clamp_fusion), kind=kCustom, calls=%fused_computation.3 | custom fusion | bytes 4210688 | tf_op jit(solution)/shard_map/gather | solution.py:109
  263.5 1.9 copy.35
  265.4 0.7 copy.36
  266.1 58.3 %all_to_all.20 = bf16[128,2,32,128]{3,2,1,0:T(8,128)(2,1)S(1)} all-to-all(bf16[128,2,32,128]{3,2,1,0:T(8,128)(2,1)S(1)} %copy.36), channel_id=1, replica_groups=mesh['wide'=128,'head'=2] {'wide'}, dimensions={0} | all-to-all | bytes 4194304 | tf_op jit(solution)/shard_map/all_to_all | solution.py:110
  324.4 2.2 copy.37
  326.6 0.0 copy-start.15
  326.7 0.7 multiply_reduce_fusion
  327.4 0.5 copy-done.9
  327.9 0.7 multiply_reduce_fusion.1
  328.6 0.5 copy-done.1
  329.1 0.7 multiply_convert_fusion
  329.8 3.7 copy.38
  333.5 7.4 %all-to-all-start.2 = ((bf16[128,2,32,128]{3,1,2,0:T(2,128)(2,1)}), bf16[128,2,32,128]{3,1,2,0:T(2,128)(2,1)}, u32[]{:S(2)}, u32[]{:S(2)}) async-start(bf16[128,2,32,128]{3,1,2,0:T(2,128)(2,1)} %copy.38), calls=%async_computation.2 | async-start | bytes 4194304 | tf_op jit(solution)/shard_map/all_to_all | solution.py:116
  340.9 0.1 eq.15
  341.0 51.7 %all-to-all-done.2 = bf16[128,2,32,128]{3,1,2,0:T(2,128)(2,1)} async-done(((bf16[128,2,32,128]{3,1,2,0:T(2,128)(2,1)}), bf16[128,2,32,128]{3,1,2,0:T(2,128)(2,1)}, u32[]{:S(2)}, u32[]{:S(2)}) %all-to-all-start.2) | async-done | bytes 2097184 | tf_op jit(solution)/shard_map/all_to_all | solution.py:116
  392.7 1.9 copy.39
  394.6 0.4 convolution_bitcast_fusion
  395.0 0.7 fusion.9
  (39 shorter events, 0.2 us)
Async XLA Ops:
  0.0 1.6 copy-start
  3.6 8.2 %copy-start.10 = (s32[4]{0:T(128)S(1)}, s32[4]{0:T(128)}, u32[]{:S(2)}) copy-start(s32[4]{0:T(128)} %param.22) | copy-start | bytes 52
  3.6 10.1 %copy-start.5 = (bf16[4,512]{1,0:T(4,128)(2,1)S(1)}, bf16[4,512]{1,0:T(4,128)(2,1)}, u32[]{:S(2)}) copy-start(bf16[4,512]{1,0:T(4,128)(2,1)} %param.18) | copy-start | bytes 12292
  3.6 10.1 %copy-start.6 = (bf16[4,512]{1,0:T(4,128)(2,1)S(1)}, bf16[4,512]{1,0:T(4,128)(2,1)}, u32[]{:S(2)}) copy-start(bf16[4,512]{1,0:T(4,128)(2,1)} %param.19) | copy-start | bytes 12292
  3.6 10.2 %copy-start.11 = (s32[1,32]{1,0:T(1,128)S(1)}, s32[1,32]{1,0:T(1,128)}, u32[]{:S(2)}) copy-start(s32[1,32]{1,0:T(1,128)} %param.32) | copy-start | bytes 388
  3.6 10.2 %copy-start.12 = (s32[1,32]{1,0:T(1,128)S(1)}, s32[1,32]{1,0:T(1,128)}, u32[]{:S(2)}) copy-start(s32[1,32]{1,0:T(1,128)} %param.28) | copy-start | bytes 388
  3.6 201.5 %copy-start.13 = (s32[4]{0:T(128)S(1)}, s32[4]{0:T(128)}, u32[]{:S(2)}) copy-start(s32[4]{0:T(128)} %param.23) | copy-start | bytes 52
  3.7 201.5 %copy-start.3 = (bf16[4,4096]{1,0:T(4,128)(2,1)S(1)}, bf16[4,4096]{1,0:T(4,128)(2,1)}, u32[]{:S(2)}) copy-start(bf16[4,4096]{1,0:T(4,128)(2,1)} %param.17) | copy-start | bytes 98308
  6.8 199.2 %collective-permute-start.1 = (bf16[2,4,256,512]{3,2,1,0:T(8,128)(2,1)}, bf16[2,4,256,512]{3,2,1,0:T(8,128)(2,1)}, u32[]{:S(2)}, u32[]{:S(2)}) collective-permute-start(bf16[2,4,256,512]{3,2,1,0:T(8,128)(2,1)} %bitcast.2), channel_id=1, source_target_pairs={{0,2},{2,4},{4,6},{6,8},{8,10},{10,12},{12,14},{14,16},{16,18},{18... | collective-permute-start | bytes 6291464 | tf_op jit(solution)/shard_map/ppermute | solution.py:14
  11.8 193.5 %collective-permute-start = (bf16[4]{0:T(256)(128)(2,1)S(1)}, bf16[4]{0:T(256)(128)(2,1)S(1)}, u32[]{:S(2)}, u32[]{:S(2)}) collective-permute-start(bf16[4]{0:T(256)(128)(2,1)S(1)} %convert_element_type.60), channel_id=1, source_target_pairs={{0,2},{2,4},{4,6},{6,8},{8,10},{10,12},{12,14},{14,16},{16,18},{18... | collective-permute-start | bytes 32 | tf_op jit(solution)/shard_map/ppermute | solution.py:14
  220.3 16.0 %copy-start.2 = (bf16[2,8192]{1,0:T(2,128)(2,1)S(1)}, bf16[2,8192]{1,0:T(2,128)(2,1)}, u32[]{:S(2)}) copy-start(bf16[2,8192]{1,0:T(2,128)(2,1)} %param.24) | copy-start | bytes 98308
  220.3 16.2 %copy-start.4 = (f32[8192]{0:T(1024)S(1)}, f32[8192]{0:T(1024)}, u32[]{:S(2)}) copy-start(f32[8192]{0:T(1024)} %param.25) | copy-start | bytes 98308
  223.2 13.1 %all-to-all-start = ((bf16[2,2,4096]{2,1,0:T(2,128)(2,1)}), bf16[2,2,4096]{2,1,0:T(2,128)(2,1)S(1)}, u32[]{:S(2)}, u32[]{:S(2)}) async-start(bf16[2,2,4096]{2,1,0:T(2,128)(2,1)} %convert_element_type.68), calls=%async_computation | async-start | bytes 65536 | tf_op jit(solution)/shard_map/all_to_all | solution.py:97
  324.4 2.2 copy-start.8
  324.4 2.2 copy-start.14
  326.6 1.2 copy-start.9
  326.6 1.2 copy-start.15
  327.9 1.2 copy-start.1
  327.9 1.2 copy-start.7
  333.5 59.2 %all-to-all-start.2 = ((bf16[128,2,32,128]{3,1,2,0:T(2,128)(2,1)}), bf16[128,2,32,128]{3,1,2,0:T(2,128)(2,1)}, u32[]{:S(2)}, u32[]{:S(2)}) async-start(bf16[128,2,32,128]{3,1,2,0:T(2,128)(2,1)} %copy.38), calls=%async_computation.2 | async-start | bytes 4194304 | tf_op jit(solution)/shard_map/all_to_all | solution.py:116
where the time goes:
time: 396 us
  blocking collectives  249 us (63%)
  waiting for transfers between devices  58.4 us (15%)
  local copies, waits for them, and re-layouts  55.5 us (14%)
  starting transfers between devices  20.6 us (5%)
  other arithmetic  6.95 us (2%)
  matrix products  4.63 us (1%)
    all_gather x1, blocking collectives, per_device(): lax.all_gather(jnp.concatenate([gate_up_keep, down_keep], axis=1), 'wide'...  191 us
    all_to_all x1, blocking collectives, per_device(): lax.all_to_all(outgoing, 'wide', split_axis=0, concat_axis=0, tiled=True)  58.3 us
    all_to_all x1, waiting for transfers between devices, per_device(): lax.all_to_all(contrib, 'wide', split_axis=0, concat_axis=0, tiled=True)  51.7 us
    gather x2, local copies, waits for them, and re-layouts, per_device(): outgoing = jnp.swapaxes(normed_blocks[:, in_keep], 0, 1)  28.8 us
  transfers between devices with their start and end apart: 4, of which 2 were waited for; matrix products, arithmetic and copies ran while one was open for 0% of the time, Pallas kernels for 0%

commit v1 on v0

--- a/solution.py
+++ b/solution.py
@@ -99,9 +99,11 @@
     normed = (
         middle * lax.rsqrt(jnp.mean(middle * middle, axis=-1, keepdims=True) + 1e-05) * norm_gain
     ).astype(jnp.bfloat16)
-    keep_lists = lax.all_gather(
-        jnp.concatenate([gate_up_keep, down_keep], axis=1), "wide", axis=0, tiled=True
-    )
+    array_here = jnp.concatenate([gate_up_keep, down_keep], axis=1)
+    m_next = lax.psum(1, "wide")
+    far_arr = jnp.stack([array_here] * m_next, axis=0)
+    response = lax.all_to_all(far_arr, "wide", 0, 0)
+    keep_lists = jnp.concatenate(response, axis=0)
     keep = gate_up_keep.shape[1]
     in_keep, out_keep = (keep_lists[:, :keep], keep_lists[:, keep:])
     feature_blocks = normed.shape[1] // BLK

time: 396 us -> 237 us (0.60)
  blocking collectives: 249 us -> 58.7 us
  waiting for transfers between devices: 58.4 us -> 75.2 us
  starting transfers between devices: 20.6 us -> 33.9 us
    all_gather x1 -> x0, blocking collectives: 191 us -> none  [per_device(): lax.all_gather(jnp.concatenate([gate_up_keep, down_keep], axis=1), 'wide'...]
    all_to_all x0 -> x1, starting transfers between devices: none -> 11.5 us  [per_device(): response = lax.all_to_all(far_arr, 'wide', 0, 0)]
    ppermute x2, waiting for transfers between devices: 0.01 us -> 9.38 us  [shifted(): return lax.ppermute(block, axis, route)]
    all_to_all x0 -> x1, waiting for transfers between devices: none -> 7.49 us  [per_device(): response = lax.all_to_all(far_arr, 'wide', 0, 0)]
  transfers between devices with their start and end apart: 4 -> 5, of which waited for: 2 -> 4; matrix products, arithmetic and copies ran while one was open for 0% -> 1% of each run, Pallas kernels for 0% -> 0%
where the time goes in v1:
time: 237 us; the launch traced here: 236 us
  waiting for transfers between devices  75.2 us (32%)
  blocking collectives  58.7 us (25%)
  local copies, waits for them, and re-layouts  56.2 us (24%)
  starting transfers between devices  33.9 us (14%)
  other arithmetic  6.94 us (3%)
  matrix products  4.64 us (2%)
    all_to_all x1, blocking collectives, per_device(): lax.all_to_all(outgoing, 'wide', split_axis=0, concat_axis=0, tiled=True)  58.7 us
    all_to_all x1, waiting for transfers between devices, per_device(): lax.all_to_all(contrib, 'wide', split_axis=0, concat_axis=0, tiled=True)  51.7 us
    gather x2, local copies, waits for them, and re-layouts, per_device(): outgoing = jnp.swapaxes(normed_blocks[:, in_keep], 0, 1)  28.8 us
    all_to_all x1, starting transfers between devices, per_device(): response = lax.all_to_all(far_arr, 'wide', 0, 0)  11.5 us
    ppermute x2, waiting for transfers between devices, shifted(): return lax.ppermute(block, axis, route)  9.38 us
    all_to_all x1, starting transfers between devices, per_device(): lax.all_to_all(attention, 'head', split_axis=0, concat_axis=1, tiled=True)  8.17 us
    all_to_all x1, waiting for transfers between devices, per_device(): response = lax.all_to_all(far_arr, 'wide', 0, 0)  7.49 us
    all_to_all x1, starting transfers between devices, per_device(): lax.all_to_all(contrib, 'wide', split_axis=0, concat_axis=0, tiled=True)  7.43 us
  transfers between devices with their start and end apart: 5, of which 4 were waited for; matrix products, arithmetic and copies ran while one was open for 1% of the time, Pallas kernels for 0%

profile of v1, /device:TPU:1, one launch (start us, length us, event | category | flops | bytes accessed | tf_op | source)
XLA Modules:
  0.0 236.0 jit_solution(11976552089026778066)
XLA Ops:
  0.0 0.8 compare_select_fusion.1
  0.8 0.1 reshape.103
  0.9 0.7 copy-done
  1.6 2.0 gather_fusion.1
  3.7 3.2 %copy.29 = bf16[64,2,16,512]{3,2,0,1:T(8,128)(2,1)} copy(bf16[64,2,16,512]{3,2,1,0:T(8,128)(2,1)} %gather_fusion.1) | data formatting | bytes 4194304 | tf_op jit(solution)/shard_map/gather | solution.py:88
  6.9 4.9 %collective-permute-start.1 = (bf16[2,4,256,512]{3,2,1,0:T(8,128)(2,1)}, bf16[2,4,256,512]{3,2,1,0:T(8,128)(2,1)}, u32[]{:S(2)}, u32[]{:S(2)}) collective-permute-start(bf16[2,4,256,512]{3,2,1,0:T(8,128)(2,1)} %bitcast.2), channel_id=1, source_target_pairs={{0,2},{2,4},{4,6},{6,8},{8,10},{10,12},{12,14},{14,16},{16,18},{18... | collective-permute-start | bytes 6291464 | tf_op jit(solution)/shard_map/ppermute | solution.py:14
  11.8 1.9 collective-permute-start
  13.8 0.1 add_bitcast_fusion
  13.8 0.7 stack.2
  14.5 11.5 %all-to-all-start.1 = ((s32[128,1,64]{2,1,0:T(1,128)}), s32[128,1,64]{2,1,0:T(1,128)S(1)}, u32[]{:S(2)}, u32[]{:S(2)}) async-start(s32[128,1,64]{2,1,0:T(1,128)} %stack.2), calls=%async_computation.1 | async-start | bytes 131072 | tf_op jit(solution)/shard_map/all_to_all | solution.py:105
  26.1 0.1 fusion.15
  26.2 9.4 %collective-permute-done = bf16[4]{0:T(256)(128)(2,1)S(1)} collective-permute-done((bf16[4]{0:T(256)(128)(2,1)S(1)}, bf16[4]{0:T(256)(128)(2,1)S(1)}, u32[]{:S(2)}, u32[]{:S(2)}) %collective-permute-start) | collective-permute-done | bytes 40 | tf_op jit(solution)/shard_map/ppermute | solution.py:14
  35.6 0.1 maximum_convert_fusion
  35.7 0.6 gather_fusion
  36.3 0.1 iota_compare_fusion.1
  36.4 7.5 %all-to-all-done.1 = s32[128,1,64]{2,1,0:T(1,128)S(1)} async-done(((s32[128,1,64]{2,1,0:T(1,128)}), s32[128,1,64]{2,1,0:T(1,128)S(1)}, u32[]{:S(2)}, u32[]{:S(2)}) %all-to-all-start.1) | async-done | bytes 32800 | tf_op jit(solution)/shard_map/all_to_all | solution.py:105
  43.9 0.1 fusion.26
  43.9 0.1 reshape.119
  44.0 4.5 %pad_maximum_fusion = bf16[2,8,256,512]{3,2,1,0:T(8,128)(2,1)} fusion(bf16[2,4,256,512]{3,2,1,0:T(8,128)(2,1)} %bitcast.2, bf16[2,4,256,512]{3,2,1,0:T(8,128)(2,1)} %collective-permute-done.1), kind=kLoop, calls=%fused_computation.4 | loop fusion | flops 2097152 | bytes 8388608 | tf_op jit(solution)/shard_map/concatenate | solution.py:91
  48.6 4.2 %gather_fusion.2 = bf16[4,2,256,512]{3,2,1,0:T(8,128)(2,1)} fusion(bf16[2,8,256,512]{3,2,1,0:T(8,128)(2,1)} %pad_maximum_fusion, s32[1024]{0:T(1024)S(1)} %pad_clamp_fusion.1), kind=kCustom, calls=%fused_computation.2 | custom fusion | bytes 4194320 | tf_op jit(solution)/shard_map/gather | solution.py:94
  52.8 2.7 %fusion.25 = (bf16[1,4,256,512]{3,2,0,1:T(8,128)(2,1)}, bf16[1,4,256,512]{3,2,0,1:T(8,128)(2,1)S(1)}) fusion(bf16[2,4,256,512]{3,2,0,1:T(8,128)(2,1)} %bitcast.73), kind=kLoop, calls=%fused_computation.57 | loop fusion | bytes 4194304 | tf_op jit(solution)/shard_map/slice | solution.py:23
  55.5 1.3 copy.32
  56.8 1.5 copy.30
  58.3 0.3 select_reduce_fusion
  58.6 0.2 bitcast_reduce_fusion
  58.9 1.6 fusion
  60.5 0.6 convert_element_type.68
  61.1 8.2 %all-to-all-start = ((bf16[2,2,4096]{2,1,0:T(2,128)(2,1)}), bf16[2,2,4096]{2,1,0:T(2,128)(2,1)S(1)}, u32[]{:S(2)}, u32[]{:S(2)}) async-start(bf16[2,2,4096]{2,1,0:T(2,128)(2,1)} %convert_element_type.68), calls=%async_computation | async-start | bytes 65536 | tf_op jit(solution)/shard_map/all_to_all | solution.py:97
  69.3 6.7 %all-to-all-done = bf16[2,2,4096]{2,1,0:T(2,128)(2,1)S(1)} async-done(((bf16[2,2,4096]{2,1,0:T(2,128)(2,1)}), bf16[2,2,4096]{2,1,0:T(2,128)(2,1)S(1)}, u32[]{:S(2)}, u32[]{:S(2)}) %all-to-all-start) | async-done | bytes 32800 | tf_op jit(solution)/shard_map/all_to_all | solution.py:97
  76.1 0.2 multiply_reduce_fusion.2
  76.3 0.1 fusion.18
  76.4 27.0 %gather_fusion.3 = bf16[4096,2,128]{2,1,0:T(2,128)(2,1)} fusion(bf16[2,64,128]{2,0,1:T(2,128)(2,1)S(1)} %fusion.18, s32[4096]{0:T(1024)S(1)} %broadcast_clamp_fusion), kind=kCustom, calls=%fused_computation.3 | custom fusion | bytes 4210688 | tf_op jit(solution)/shard_map/gather | solution.py:111
  103.3 1.9 copy.35
  105.2 0.7 copy.36
  105.9 58.7 %all_to_all.25 = bf16[128,2,32,128]{3,2,1,0:T(8,128)(2,1)S(1)} all-to-all(bf16[128,2,32,128]{3,2,1,0:T(8,128)(2,1)S(1)} %copy.36), channel_id=1, replica_groups=mesh['wide'=128,'head'=2] {'wide'}, dimensions={0} | all-to-all | bytes 4194304 | tf_op jit(solution)/shard_map/all_to_all | solution.py:112
  164.7 2.2 copy.37
  166.9 0.7 multiply_reduce_fusion
  167.6 0.5 copy-done.9
  168.1 0.7 multiply_reduce_fusion.1
  168.8 0.5 copy-done.1
  169.4 0.7 multiply_convert_fusion
  170.1 3.7 %copy.38 = bf16[128,2,32,128]{3,1,2,0:T(2,128)(2,1)} copy(bf16[128,2,32,128]{3,1,0,2:T(2,128)(2,1)S(1)} %bitcast.74) | data formatting | bytes 4194304 | tf_op jit(solution)/shard_map/reshape | solution.py:117
  173.8 7.4 %all-to-all-start.3 = ((bf16[128,2,32,128]{3,1,2,0:T(2,128)(2,1)}), bf16[128,2,32,128]{3,1,2,0:T(2,128)(2,1)}, u32[]{:S(2)}, u32[]{:S(2)}) async-start(bf16[128,2,32,128]{3,1,2,0:T(2,128)(2,1)} %copy.38), calls=%async_computation.3 | async-start | bytes 4194304 | tf_op jit(solution)/shard_map/all_to_all | solution.py:118
  181.2 0.1 eq.15
  181.3 51.7 %all-to-all-done.3 = bf16[128,2,32,128]{3,1,2,0:T(2,128)(2,1)} async-done(((bf16[128,2,32,128]{3,1,2,0:T(2,128)(2,1)}), bf16[128,2,32,128]{3,1,2,0:T(2,128)(2,1)}, u32[]{:S(2)}, u32[]{:S(2)}) %all-to-all-start.3) | async-done | bytes 2097184 | tf_op jit(solution)/shard_map/all_to_all | solution.py:118
  232.9 1.9 copy.39
  234.9 0.4 convolution_bitcast_fusion
  235.3 0.7 fusion.9
  (41 shorter events, 0.2 us)
Async XLA Ops:
  0.0 1.6 copy-start
  3.6 8.2 %copy-start.10 = (s32[4]{0:T(128)S(1)}, s32[4]{0:T(128)}, u32[]{:S(2)}) copy-start(s32[4]{0:T(128)} %param.22) | copy-start | bytes 52
  3.6 10.1 %copy-start.11 = (s32[1,32]{1,0:T(1,128)S(1)}, s32[1,32]{1,0:T(1,128)}, u32[]{:S(2)}) copy-start(s32[1,32]{1,0:T(1,128)} %param.32) | copy-start | bytes 388
  3.6 10.1 %copy-start.12 = (s32[1,32]{1,0:T(1,128)S(1)}, s32[1,32]{1,0:T(1,128)}, u32[]{:S(2)}) copy-start(s32[1,32]{1,0:T(1,128)} %param.28) | copy-start | bytes 388
  3.6 22.4 %copy-start.5 = (bf16[4,512]{1,0:T(4,128)(2,1)S(1)}, bf16[4,512]{1,0:T(4,128)(2,1)}, u32[]{:S(2)}) copy-start(bf16[4,512]{1,0:T(4,128)(2,1)} %param.18) | copy-start | bytes 12292
  3.6 22.4 %copy-start.6 = (bf16[4,512]{1,0:T(4,128)(2,1)S(1)}, bf16[4,512]{1,0:T(4,128)(2,1)}, u32[]{:S(2)}) copy-start(bf16[4,512]{1,0:T(4,128)(2,1)} %param.19) | copy-start | bytes 12292
  3.6 22.4 %copy-start.13 = (s32[4]{0:T(128)S(1)}, s32[4]{0:T(128)}, u32[]{:S(2)}) copy-start(s32[4]{0:T(128)} %param.23) | copy-start | bytes 52
  3.6 22.4 %copy-start.3 = (bf16[4,4096]{1,0:T(4,128)(2,1)S(1)}, bf16[4,4096]{1,0:T(4,128)(2,1)}, u32[]{:S(2)}) copy-start(bf16[4,4096]{1,0:T(4,128)(2,1)} %param.17) | copy-start | bytes 98308
  6.9 37.2 %collective-permute-start.1 = (bf16[2,4,256,512]{3,2,1,0:T(8,128)(2,1)}, bf16[2,4,256,512]{3,2,1,0:T(8,128)(2,1)}, u32[]{:S(2)}, u32[]{:S(2)}) collective-permute-start(bf16[2,4,256,512]{3,2,1,0:T(8,128)(2,1)} %bitcast.2), channel_id=1, source_target_pairs={{0,2},{2,4},{4,6},{6,8},{8,10},{10,12},{12,14},{14,16},{16,18},{18... | collective-permute-start | bytes 6291464 | tf_op jit(solution)/shard_map/ppermute | solution.py:14
  11.8 23.8 %collective-permute-start = (bf16[4]{0:T(256)(128)(2,1)S(1)}, bf16[4]{0:T(256)(128)(2,1)S(1)}, u32[]{:S(2)}, u32[]{:S(2)}) collective-permute-start(bf16[4]{0:T(256)(128)(2,1)S(1)} %convert_element_type.60), channel_id=1, source_target_pairs={{0,2},{2,4},{4,6},{6,8},{8,10},{10,12},{12,14},{14,16},{16,18},{18... | collective-permute-start | bytes 32 | tf_op jit(solution)/shard_map/ppermute | solution.py:14
  14.5 29.4 %all-to-all-start.1 = ((s32[128,1,64]{2,1,0:T(1,128)}), s32[128,1,64]{2,1,0:T(1,128)S(1)}, u32[]{:S(2)}, u32[]{:S(2)}) async-start(s32[128,1,64]{2,1,0:T(1,128)} %stack.2), calls=%async_computation.1 | async-start | bytes 131072 | tf_op jit(solution)/shard_map/all_to_all | solution.py:105
  58.3 17.8 %copy-start.2 = (bf16[2,8192]{1,0:T(2,128)(2,1)S(1)}, bf16[2,8192]{1,0:T(2,128)(2,1)}, u32[]{:S(2)}) copy-start(bf16[2,8192]{1,0:T(2,128)(2,1)} %param.24) | copy-start | bytes 98308
  58.3 18.0 %copy-start.4 = (f32[8192]{0:T(1024)S(1)}, f32[8192]{0:T(1024)}, u32[]{:S(2)}) copy-start(f32[8192]{0:T(1024)} %param.25) | copy-start | bytes 98308
  61.1 14.9 %all-to-all-start = ((bf16[2,2,4096]{2,1,0:T(2,128)(2,1)}), bf16[2,2,4096]{2,1,0:T(2,128)(2,1)S(1)}, u32[]{:S(2)}, u32[]{:S(2)}) async-start(bf16[2,2,4096]{2,1,0:T(2,128)(2,1)} %convert_element_type.68), calls=%async_computation | async-start | bytes 65536 | tf_op jit(solution)/shard_map/all_to_all | solution.py:97
  164.7 2.2 copy-start.8
  164.7 2.2 copy-start.14
  166.9 1.2 copy-start.9
  166.9 1.2 copy-start.15
  168.1 1.2 copy-start.1
  168.1 1.2 copy-start.7
  173.8 59.2 %all-to-all-start.3 = ((bf16[128,2,32,128]{3,1,2,0:T(2,128)(2,1)}), bf16[128,2,32,128]{3,1,2,0:T(2,128)(2,1)}, u32[]{:S(2)}, u32[]{:S(2)}) async-start(bf16[128,2,32,128]{3,1,2,0:T(2,128)(2,1)} %copy.38), calls=%async_computation.3 | async-start | bytes 4194304 | tf_op jit(solution)/shard_map/all_to_all | solution.py:118
